TPU v7x, 512 devices: a whole 4x4x16 slice. The times are simulated.
512 devices in a mesh: row: 16 (over z), col: 8 (over x, core), layer: 4 (over y).
Axes of the slice: x: 4, y: 4, z: 16, core: 2. Of those that a mesh axis runs over, the one named last changes fastest.
Arguments:
- p_slabs: bfloat16 [4, 4096, 1024], P('layer', 'row', 'col'), may hold values from -0.09375 to 0.09375
- p_mask: int32 [4, 128, 32], P('layer', 'row', 'col'), may hold values 0 or 1
- h_slabs: bfloat16 [4, 1024, 4096], P('layer', 'row', 'col'), may hold values from -12 to 12
- h_mask: int32 [4, 32, 128], P('layer', 'row', 'col'), may hold values from 0 to 1, as said below
- gauss_row: int32 [524288], P(('row', 'col', 'layer')), may hold values from 0 to 255
- gauss_col: int32 [524288], P(('row', 'col', 'layer')), may hold values from 0 to 4095
- gauss_cell: int32 [524288], P(('row', 'col', 'layer')), may hold values from 0 to 32767
- gauss_expo: float32 [524288], P(('row', 'col', 'layer')), may hold values from 0.05 to 0.6
- gauss_pref: float32 [524288], P(('row', 'col', 'layer')), may hold values from -384 to 384
Outputs:
- product: bfloat16 [4096, 4096], P('row', ('col', 'layer'))
- density: float32 [256, 128, 512], P('row', 'col', 'layer')
Inputs may be any that keep to these rules, and one draw needn't show every extreme that they name: Each device's tile of h_mask (block rows l, r * 2 to r * 2 + 1, block columns c * 16 to c * 16 + 15) has at most 16 ones; some tile has exactly 16.
All inputs are finite; a program needn't handle non-finite values. No bound on the sum of `p_mask` on one device may be relied on, other than what follows from the above.
Results may differ from a plain program's by a relative error of at most 0.001.
Values may be sent and summed in bfloat16 or wider, within the bound.
A program may use at most 64 MiB of HBM per device.

v0:
```python
import jax
import jax.numpy as jnp
from jax import lax
from jax.sharding import PartitionSpec as P

BS = 32
GX = 16
GY = 16
GZ = 128
R = 4


def with_halo(block, sides, width):
    for axis, dim in sides:
        count = lax.axis_size(axis)
        forward = [(i, i + 1) for i in range(count - 1)]
        forward.append((count - 1, 0))
        backward = [(target, source) for source, target in forward]
        low = lax.ppermute(
            lax.slice_in_dim(block, block.shape[dim] - width, None, axis=dim), axis, forward
        )
        high = lax.ppermute(lax.slice_in_dim(block, 0, width, axis=dim), axis, backward)
        block = jnp.concatenate([low, block, high], axis=dim)
    return block


def expand_mask(mask, block):
    return jnp.repeat(jnp.repeat(mask, block, axis=0), block, axis=1) > 0


def profile(center, expo, length):
    pos = jnp.arange(length + 2 * R, dtype=jnp.int32) - R
    dist = pos[:, None] - center[None, :]
    dist_f = dist.astype(jnp.float32)
    value = jnp.exp(-expo[None, :] * dist_f * dist_f)
    return jnp.where(jnp.abs(dist) <= R, value, jnp.zeros_like(value))


def collocate(cell, expo, coef, size_x, size_y, size_z):
    cx = cell // (size_y * size_z)
    cy = cell // size_z % size_y
    cz = cell % size_z
    ex = profile(cx, expo, size_x)
    ey = profile(cy, expo, size_y)
    ez = profile(cz, expo, size_z)
    plane = (ex[:, None, :] * ey[None, :, :]).reshape((size_x + 2 * R) * (size_y + 2 * R), -1)
    depth = ez * coef[None, :]
    dens = lax.dot_general(
        plane,
        depth,
        (((1,), (1,)), ((), ())),
        precision=lax.Precision.HIGHEST,
        preferred_element_type=jnp.float32,
    )
    return dens.reshape(size_x + 2 * R, size_y + 2 * R, size_z + 2 * R)


def fold_rims(extended, axis, cells):
    core = lax.slice_in_dim(extended, 2 * R, 2 * R + cells, axis=axis)
    low = lax.slice_in_dim(extended, 0, R, axis=axis)
    high = lax.slice_in_dim(extended, cells + 3 * R, cells + 4 * R, axis=axis)
    widths_low = [(0, 0)] * extended.ndim
    widths_low[axis] = (0, cells - R)
    widths_high = [(0, 0)] * extended.ndim
    widths_high[axis] = (cells - R, 0)
    return core + jnp.pad(low, widths_low) + jnp.pad(high, widths_high)


def on_device(
    p_slabs, p_mask, h_slabs, h_mask, gauss_row, gauss_col, gauss_cell, gauss_expo, gauss_pref
):
    p_local = p_slabs[0]
    p_local = jnp.where(expand_mask(p_mask[0], BS), p_local, jnp.zeros_like(p_local))
    p_whole = lax.all_gather(p_local, "col", axis=1, tiled=True)
    p_rows = lax.all_gather(p_whole, "layer", axis=1, tiled=True)
    h_local = h_slabs[0]
    h_pattern = h_mask[0]
    h_eff = jnp.where(expand_mask(h_pattern, BS), h_local, jnp.zeros_like(h_local))
    h_slab = lax.all_gather(h_eff, "row", axis=0, tiled=True)
    h_inner = lax.all_to_all(h_slab, "layer", split_axis=1, concat_axis=0, tiled=True)
    summed = jnp.dot(p_rows, h_inner, preferred_element_type=jnp.float32)
    product = summed.astype(jnp.bfloat16)
    coef = gauss_pref * p_rows[gauss_row, gauss_col].astype(jnp.float32)
    padded = collocate(gauss_cell, gauss_expo, coef, GX, GY, GZ)
    extended = with_halo(padded, (("row", 0), ("col", 1), ("layer", 2)), R)
    density = fold_rims(extended, 0, GX)
    density = fold_rims(density, 1, GY)
    density = fold_rims(density, 2, GZ)
    return (product, density)


def solution(mesh):
    placed = (
        P("layer", "row", "col"),
        P("layer", "row", "col"),
        P("layer", "row", "col"),
        P("layer", "row", "col"),
        P(("row", "col", "layer")),
        P(("row", "col", "layer")),
        P(("row", "col", "layer")),
        P(("row", "col", "layer")),
        P(("row", "col", "layer")),
    )
    return jax.shard_map(
        on_device,
        mesh=mesh,
        in_specs=placed,
        out_specs=(P("row", ("col", "layer")), P("row", "col", "layer")),
        check_vma=False,
    )
```

profile of v0, /device:TPU:1, one launch (start us, length us, event | category | flops | bytes accessed | tf_op | source)
XLA Modules:
  0.0 187.6 jit_solution(672247300092082419)
XLA Ops:
  7.2 0.0 all-gather.5.cloned.1.call-start
  7.2 0.7 compare_bitcast_fusion
  7.9 0.1 copy.37
  8.0 0.1 broadcast_in_dim.42
  8.1 0.1 gt.42
  8.2 1.0 copy.38
  9.2 0.7 copy.39
  9.9 0.0 all-gather.5.cloned.1.call-update
  9.9 0.0 all-gather.3.cloned.1.call-start
  10.0 0.7 compare_bitcast_fusion.1
  10.7 0.1 broadcast_in_dim.18
  10.7 0.1 gt.37
  10.8 0.1 copy.36
  11.0 0.9 bitcast_select_fusion.1
  11.8 19.6 %all_gather.9 = bf16[256,1024]{1,0:T(8,128)(2,1)} all-gather(bf16[256,128]{1,0:T(8,128)(2,1)S(1)} %bitcast_select_fusion.1), channel_id=1, replica_groups=mesh['row'=16,'col'=8,'layer'=4] {'col'}, dimensions={1}, use_global_device_ids=true | all-gather | bytes 589824 | tf_op jit(solution)/shard_map/all_gather | solution.py:74
  31.4 0.0 all-gather.3.cloned.1.call-update
  31.4 0.7 neg.6
  32.1 0.7 fusion.38
  32.8 0.7 add_select_fusion
  33.5 0.1 fusion.31
  33.7 0.3 broadcast_multiply_fusion
  34.0 42.3 %all-gather.5.cloned.1.call-done = bf16[1024,512]{1,0:T(8,128)(2,1)} async-done(((bf16[64,512]{1,0:T(8,128)(2,1)}), bf16[1024,512]{1,0:T(8,128)(2,1)}) %all-gather.5.cloned.1.call-update) | async-done | bytes 1048592 | tf_op jit(solution)/shard_map/all_gather | solution.py:79
  76.3 2.3 %copy.40 = bf16[1024,512]{0,1:T(8,128)(2,1)} copy(bf16[1024,512]{1,0:T(8,128)(2,1)} %all-gather.5.cloned.1.call-done) | data formatting | bytes 2097152 | tf_op jit(solution)/shard_map/all_gather | solution.py:79
  78.5 0.0 copy-start.2
  78.5 4.1 %all-to-all-start = ((bf16[1024,4,128]{0,2,1:T(8,128)(2,1)}), bf16[1024,4,128]{0,2,1:T(8,128)(2,1)S(1)}, u32[]{:S(2)}, u32[]{:S(2)}) async-start(bf16[1024,4,128]{0,2,1:T(8,128)(2,1)} %bitcast.32), calls=%async_computation | async-start | bytes 2097152 | tf_op jit(solution)/shard_map/all_to_all | solution.py:80
  82.7 41.4 %all-gather.3.cloned.1.call-done = bf16[256,4096]{1,0:T(8,128)(2,1)} async-done(((bf16[256,1024]{1,0:T(8,128)(2,1)}), bf16[256,4096]{1,0:T(8,128)(2,1)}) %all-gather.3.cloned.1.call-update) | async-done | bytes 2097168 | tf_op jit(solution)/shard_map/all_gather | solution.py:75
  124.1 13.1 %gather_fusion = bf16[1024]{0:T(1024)(128)(2,1)S(1)} fusion(bf16[256,4096]{1,0:T(8,128)(2,1)} %all-gather.3.cloned.1.call-done, s32[1024]{0:T(1024)S(1)} %fusion.38), kind=kCustom, calls=%fused_computation | custom fusion | bytes 12288 | tf_op jit(solution)/shard_map/gather | solution.py:83
  137.1 0.0 copy-done.2
  137.2 2.8 %fusion.4 = f32[576,136]{0,1:T(8,128)S(1)} fusion(f32[576,1024]{1,0:T(8,128)S(1)} %bitcast.29, f32[1024]{0:T(1024)S(1)} %convert_multiply_fusion, f32[1024]{0:T(1024)S(1)} %neg.6, s32[1024]{0:T(1024)S(1)} %get-tuple-element.10, s32[136]{0:T(256)S(1)} %iota_add_fusion), kind=kOutput, calls=%fused_computation.12 | convolution fusion | flops 963706880 | bytes 2685472 | tf_op jit(solution)/shard_map/dot_general | solution.py:48
  139.9 0.0 copy-start.1
  139.9 0.7 copy-done.1
  140.7 0.1 fusion.46
  140.7 0.1 copy.42
  140.8 0.1 copy.44
  140.9 5.7 %collective-permute-start.1 = (f32[4,24,136]{2,1,0:T(8,128)S(1)}, f32[4,24,136]{2,1,0:T(8,128)S(1)}, u32[]{:S(2)}, u32[]{:S(2)}) collective-permute-start(f32[4,24,136]{2,1,0:T(8,128)S(1)} %bitcast.35), channel_id=1, source_target_pairs={{32,0},{64,32},{96,64},{128,96},{160,128},{192,160},{224,192},{256... | collective-permute-start | bytes 156680 | tf_op jit(solution)/shard_map/ppermute | solution.py:22
  146.6 1.9 %collective-permute-start = (f32[4,24,136]{2,1,0:T(8,128)S(1)}, f32[4,24,136]{2,1,0:T(8,128)S(1)}, u32[]{:S(2)}, u32[]{:S(2)}) collective-permute-start(f32[4,24,136]{2,1,0:T(8,128)S(1)} %bitcast.34), channel_id=1, source_target_pairs={{0,32},{32,64},{64,96},{96,128},{128,160},{160,192},{192,224},{224... | collective-permute-start | bytes 156680 | tf_op jit(solution)/shard_map/ppermute | solution.py:19
  148.5 1.2 copy.43
  149.7 0.0 collective-permute-done.1
  149.7 3.4 %collective-permute-done = f32[4,24,136]{2,1,0:T(8,128)S(1)} collective-permute-done((f32[4,24,136]{2,1,0:T(8,128)S(1)}, f32[4,24,136]{2,1,0:T(8,128)S(1)}, u32[]{:S(2)}, u32[]{:S(2)}) %collective-permute-start) | collective-permute-done | bytes 52256 | tf_op jit(solution)/shard_map/ppermute | solution.py:19
  153.2 0.1 pad_maximum_fusion.4
  153.2 3.4 %collective-permute-start.2 = (f32[32,4,136]{2,1,0:T(4,128)S(1)}, f32[32,4,136]{2,1,0:T(4,128)S(1)}, u32[]{:S(2)}, u32[]{:S(2)}) collective-permute-start(f32[32,4,136]{2,1,0:T(4,128)S(1)} %get-tuple-element.4), channel_id=1, source_target_pairs={{0,4},{4,8},{8,12},{12,16},{16,20},{20,24},{24,28},{28,0},{1,5},{5... | collective-permute-start | bytes 208904 | tf_op jit(solution)/shard_map/ppermute | solution.py:19
  156.6 0.0 collective-permute-start.3
  156.6 0.0 all-to-all-done
  156.6 0.7 copy.41
  157.3 0.0 copy-start
  157.3 1.3 collective-permute-done.2
  158.6 2.4 %collective-permute-done.3 = f32[32,4,136]{2,1,0:T(4,128)S(1)} collective-permute-done((f32[32,4,136]{2,1,0:T(4,128)S(1)}, f32[32,4,136]{2,1,0:T(4,128)S(1)}, u32[]{:S(2)}, u32[]{:S(2)}) %collective-permute-start.3) | collective-permute-done | bytes 69664 | tf_op jit(solution)/shard_map/ppermute | solution.py:22
  161.0 0.2 pad_maximum_fusion
  161.2 0.2 fusion.45
  161.4 2.2 %collective-permute-start.4 = (f32[32,32,4]{2,1,0:T(8,128)S(1)}, f32[32,32,4]{2,1,0:T(8,128)S(1)}, u32[]{:S(2)}, u32[]{:S(2)}) collective-permute-start(f32[32,32,4]{2,1,0:T(8,128)S(1)} %get-tuple-element.2), channel_id=1, source_target_pairs={{0,1},{1,2},{2,3},{3,0},{4,5},{5,6},{6,7},{7,4},{8,9},{9,10},{10,1... | collective-permute-start | bytes 49160 | tf_op jit(solution)/shard_map/ppermute | solution.py:19
  163.6 4.3 %collective-permute-start.5 = (f32[32,32,4]{2,1,0:T(8,128)S(1)}, f32[32,32,4]{2,1,0:T(8,128)S(1)}, u32[]{:S(2)}, u32[]{:S(2)}) collective-permute-start(f32[32,32,4]{2,1,0:T(8,128)S(1)} %get-tuple-element.3), channel_id=1, source_target_pairs={{1,0},{2,1},{3,2},{0,3},{5,4},{6,5},{7,6},{4,7},{9,8},{10,9},{11,1... | collective-permute-start | bytes 49160 | tf_op jit(solution)/shard_map/ppermute | solution.py:22
  167.9 0.0 copy-done
  167.9 1.3 convolution_convert_fusion
  169.3 0.0 copy-start.3
  169.3 8.5 %collective-permute-done.4 = f32[32,32,4]{2,1,0:T(8,128)S(1)} collective-permute-done((f32[32,32,4]{2,1,0:T(8,128)S(1)}, f32[32,32,4]{2,1,0:T(8,128)S(1)}, u32[]{:S(2)}, u32[]{:S(2)}) %collective-permute-start.4) | collective-permute-done | bytes 16416 | tf_op jit(solution)/shard_map/ppermute | solution.py:19
  177.8 0.9 collective-permute-done.5
  178.7 0.6 pad_maximum_fusion.1
  179.3 0.0 copy-done.3
  179.3 0.0 copy-start.4
  179.3 0.2 fusion.7
  179.5 0.1 fusion.25
  179.7 0.1 slice.84
  179.8 0.2 copy-done.4
  180.0 0.8 fusion.27
  (6 shorter events, 0.1 us)
Async XLA Ops:
  7.2 69.1 %all-gather.5.cloned.1.call-start = ((), (), s32[]{:S(2)}) async-start(), calls=%async_computation.2 | async-start | bytes 1114112 | tf_op jit(solution)/shard_map/all_gather | solution.py:79
  9.9 114.1 %all-gather.3.cloned.1.call-start = ((), (), s32[]{:S(2)}) async-start(), calls=%async_computation.1 | async-start | bytes 2621440 | tf_op jit(solution)/shard_map/all_gather | solution.py:75
  78.5 58.6 %copy-start.2 = (f32[1024]{0:T(1024)S(1)}, f32[1024]{0:T(1024)}, u32[]{:S(2)}) copy-start(f32[1024]{0:T(1024)} %param.17) | copy-start | bytes 12292
  78.5 78.1 %all-to-all-start = ((bf16[1024,4,128]{0,2,1:T(8,128)(2,1)}), bf16[1024,4,128]{0,2,1:T(8,128)(2,1)S(1)}, u32[]{:S(2)}, u32[]{:S(2)}) async-start(bf16[1024,4,128]{0,2,1:T(8,128)(2,1)} %bitcast.32), calls=%async_computation | async-start | bytes 2097152 | tf_op jit(solution)/shard_map/all_to_all | solution.py:80
  139.9 0.7 copy-start.1
  140.9 8.8 %collective-permute-start.1 = (f32[4,24,136]{2,1,0:T(8,128)S(1)}, f32[4,24,136]{2,1,0:T(8,128)S(1)}, u32[]{:S(2)}, u32[]{:S(2)}) collective-permute-start(f32[4,24,136]{2,1,0:T(8,128)S(1)} %bitcast.35), channel_id=1, source_target_pairs={{32,0},{64,32},{96,64},{128,96},{160,128},{192,160},{224,192},{256... | collective-permute-start | bytes 156680 | tf_op jit(solution)/shard_map/ppermute | solution.py:22
  146.6 6.6 %collective-permute-start = (f32[4,24,136]{2,1,0:T(8,128)S(1)}, f32[4,24,136]{2,1,0:T(8,128)S(1)}, u32[]{:S(2)}, u32[]{:S(2)}) collective-permute-start(f32[4,24,136]{2,1,0:T(8,128)S(1)} %bitcast.34), channel_id=1, source_target_pairs={{0,32},{32,64},{64,96},{96,128},{128,160},{160,192},{192,224},{224... | collective-permute-start | bytes 156680 | tf_op jit(solution)/shard_map/ppermute | solution.py:19
  153.2 5.3 %collective-permute-start.2 = (f32[32,4,136]{2,1,0:T(4,128)S(1)}, f32[32,4,136]{2,1,0:T(4,128)S(1)}, u32[]{:S(2)}, u32[]{:S(2)}) collective-permute-start(f32[32,4,136]{2,1,0:T(4,128)S(1)} %get-tuple-element.4), channel_id=1, source_target_pairs={{0,4},{4,8},{8,12},{12,16},{16,20},{20,24},{24,28},{28,0},{1,5},{5... | collective-permute-start | bytes 208904 | tf_op jit(solution)/shard_map/ppermute | solution.py:19
  156.6 4.4 %collective-permute-start.3 = (f32[32,4,136]{2,1,0:T(4,128)S(1)}, f32[32,4,136]{2,1,0:T(4,128)S(1)}, u32[]{:S(2)}, u32[]{:S(2)}) collective-permute-start(f32[32,4,136]{2,1,0:T(4,128)S(1)} %get-tuple-element.5), channel_id=1, source_target_pairs={{4,0},{8,4},{12,8},{16,12},{20,16},{24,20},{28,24},{0,28},{5,1},{9... | collective-permute-start | bytes 208904 | tf_op jit(solution)/shard_map/ppermute | solution.py:22
  157.3 10.6 %copy-start = (bf16[256,4096]{1,0:T(8,128)(2,1)S(1)}, bf16[256,4096]{1,0:T(8,128)(2,1)}, u32[]{:S(2)}) copy-start(bf16[256,4096]{1,0:T(8,128)(2,1)} %all-gather.3.cloned.1.call-done) | copy-start | bytes 6291460
  161.4 16.4 %collective-permute-start.4 = (f32[32,32,4]{2,1,0:T(8,128)S(1)}, f32[32,32,4]{2,1,0:T(8,128)S(1)}, u32[]{:S(2)}, u32[]{:S(2)}) collective-permute-start(f32[32,32,4]{2,1,0:T(8,128)S(1)} %get-tuple-element.2), channel_id=1, source_target_pairs={{0,1},{1,2},{2,3},{3,0},{4,5},{5,6},{6,7},{7,4},{8,9},{9,10},{10,1... | collective-permute-start | bytes 49160 | tf_op jit(solution)/shard_map/ppermute | solution.py:19
  163.6 15.1 %collective-permute-start.5 = (f32[32,32,4]{2,1,0:T(8,128)S(1)}, f32[32,32,4]{2,1,0:T(8,128)S(1)}, u32[]{:S(2)}, u32[]{:S(2)}) collective-permute-start(f32[32,32,4]{2,1,0:T(8,128)S(1)} %get-tuple-element.3), channel_id=1, source_target_pairs={{1,0},{2,1},{3,2},{0,3},{5,4},{6,5},{7,6},{4,7},{9,8},{10,9},{11,1... | collective-permute-start | bytes 49160 | tf_op jit(solution)/shard_map/ppermute | solution.py:22
  169.3 10.1 %copy-start.3 = (pred[16]{0:T(512)(128)(4,1)S(1)}, pred[16]{0:T(512)(128)(4,1)}, u32[]{:S(2)}) copy-start(pred[16]{0:T(512)(128)(4,1)} %constant.76.clone.1) | copy-start | bytes 52
  179.3 0.7 copy-start.4
Sparse Core Ops, SparseCore 0:
  10.6 65.6 all-gather.4
  78.4 45.6 all-gather.2
where the time goes:
time: 189 us; the launch traced here: 188 us
  waiting for transfers between devices  100 us (53%)
  starting transfers between devices  21.7 us (11%)
  local copies, waits for them, and re-layouts  21 us (11%)
  blocking collectives  19.6 us (10%)
  between operations  14.3 us (8%)
  other arithmetic  6.68 us (4%)
  matrix products  4.1 us (2%)
    all_gather x1, waiting for transfers between devices, on_device(): h_slab = lax.all_gather(h_eff, 'row', axis=0, tiled=True)  42.3 us
    all_gather x1, waiting for transfers between devices, on_device(): p_rows = lax.all_gather(p_whole, 'layer', axis=1, tiled=True)  41.4 us
    all_gather x1, blocking collectives, on_device(): p_whole = lax.all_gather(p_local, 'col', axis=1, tiled=True)  19.6 us
    ppermute x3, waiting for transfers between devices, with_halo(): lax.ppermute(lax.slice_in_dim(block, block.shape[dim] - width, None, axis...  13.2 us
    gather x1, local copies, waits for them, and re-layouts, on_device(): coef = gauss_pref * p_rows[gauss_row, gauss_col].astype(jnp.float32)  13.1 us
    ppermute x3, starting transfers between devices, with_halo(): lax.ppermute(lax.slice_in_dim(block, 0, width, axis=dim), axis, backward)  9.99 us
    ppermute x3, starting transfers between devices, with_halo(): lax.ppermute(lax.slice_in_dim(block, block.shape[dim] - width, None, axis...  7.45 us
    all_to_all x1, starting transfers between devices, on_device(): lax.all_to_all(h_slab, 'layer', split_axis=1, concat_axis=0, tiled=True)  4.13 us
  transfers between devices with their start and end apart: 9, of which 7 were waited for; matrix products, arithmetic and copies ran while one was open for 14% of the time, Pallas kernels for 0%

commit v1 on v0

v1 whole, which is shorter than its diff:
```python
import jax
import jax.numpy as jnp
from jax import lax
from jax.experimental import pallas as pl
from jax.experimental.pallas import tpu as pltpu
from jax.sharding import PartitionSpec as P

BS = 32
GX = 16
GY = 16
GZ = 128
R = 4
NG = 1024
NR = 16
NC = 8
NL = 4
EX = GX + 2 * R
EY = GY + 2 * R
F32 = jnp.float32
BF16 = jnp.bfloat16


def kernel(
    p_ref, h_ref, g_ref, prod_ref, dens_ref,
    pall, hall, gpad, gcols, onehot, colb, acc, ez, plane_hi, plane_lo, dens, rim, rim_in, row_in, col_in,
    send, recv, local,
):
    r = lax.axis_index("row")
    c = lax.axis_index("col")
    l = lax.axis_index("layer")
    row_of = lambda d: lax.rem(r + (d + NR), NR)
    col_of = lambda d: lax.rem(c + (d + NC), NC)
    lay_of = lambda d: lax.rem(l + (d + NL), NL)
    odd = lax.rem(c, 2)
    sib = c + 1 - 2 * odd
    out = c - 1 + 2 * odd
    other = lax.rem(out + NC, NC)

    barrier = pltpu.get_barrier_semaphore()
    peers = (
        [{"layer": lay_of(d)} for d in (1, 2, 3)]
        + [{"col": col_of(2 * d)} for d in (1, 2, 3)]
        + [{"col": sib}, {"col": other}, {"row": row_of(1)}, {"row": row_of(-1)}]
    )
    for peer in peers:
        pl.semaphore_signal(barrier, inc=1, device_id=peer, device_id_type=pl.DeviceIdType.MESH)
    pl.semaphore_wait(barrier, len(peers))

    pending = []
    slots = {}

    def push(key, src, dst, peer):
        n = slots.setdefault(key, len(slots))
        copy = pltpu.make_async_remote_copy(
            src_ref=src, dst_ref=dst, send_sem=send.at[n], recv_sem=recv.at[n],
            device_id=peer, device_id_type=pl.DeviceIdType.MESH,
        )
        copy.start()
        pending.append(copy)
        return copy

    low = pl.ds(0, 128)
    high = pl.ds(128, 128)
    copies = {}
    own_p = pltpu.make_async_copy(p_ref, pall.at[c, l], local.at[0])
    own_p.start()
    own_h = pltpu.make_async_copy(h_ref.at[l], hall.at[l, r], local.at[1])
    own_h.start()
    for d in (1, 3, 2):
        copies["ha", d] = push(("ha", d), h_ref.at[lay_of(d)], hall.at[l, r], {"layer": lay_of(d)})
    for d in (1, 3, 2):
        copies["py", d] = push(("py", d), p_ref, pall.at[c, l], {"layer": lay_of(d)})
        copies["px", d] = push(("px", d), p_ref, pall.at[c, l], {"col": col_of(2 * d)})
    copies["ps"] = push(("ps",), p_ref, pall.at[c, l], {"col": sib})

    gpad[0:8, :] = g_ref[...]
    gpad[8:128, :] = jnp.zeros((120, NG), F32)
    for k in range(NG // 128):
        gcols[k * 128 : (k + 1) * 128, :] = jnp.transpose(gpad[0:128, k * 128 : (k + 1) * 128])

    def prepare(k, _):
        rows = pl.ds(pl.multiple_of(k * 128, 128), 128)
        g = gcols[rows, :]
        lane = lax.broadcasted_iota(jnp.int32, (128, 256), 1)
        onehot[rows, :] = jnp.where(g[:, 0:1] == lane.astype(F32), 1.0, 0.0).astype(BF16)
        colb[rows, :] = g[:, 1:2] - lane[:, :128].astype(F32)
        pos = jnp.where(lane < 136, lane, lane - 144).astype(F32)
        dist = pos - g[:, 2:3]
        keep = (jnp.abs(dist) <= R) & ((lane < 132) | ((lane >= 140) & (lane < 144)))
        ez[rows, :] = jnp.where(keep, jnp.exp(-g[:, 3:4] * dist * dist), 0.0)
        acc[rows, :] = jnp.zeros((128, 128), F32)
        return 0

    lax.fori_loop(0, NG // 128, prepare, 0)

    own_h.wait()
    for d in (1, 3, 2):
        copies["ha", d].wait_recv()
    right = {"row": row_of(1)}
    left = {"row": row_of(-1)}
    copies["hr", 0] = push(("hr", 0), hall.at[:, r], hall.at[:, r], right)
    copies["hl", 0] = push(("hl", 0), hall.at[:, r], hall.at[:, r], left)

    def ring(s):
        copies["hr", s - 1].wait_recv()
        if s < NR // 2:
            piece = hall.at[:, row_of(-s)]
            copies["hr", s] = push(("hr", s), piece, piece, right)
        if s < NR // 2:
            copies["hl", s - 1].wait_recv()
        if s < NR // 2 - 1:
            piece = hall.at[:, row_of(s)]
            copies["hl", s] = push(("hl", s), piece, piece, left)

    def lookup(tiles):
        refs = [(pall.at[a, b], (b * NG + a * 128).astype(F32)) for a, b in tiles]

        def body(k, _):
            rows = pl.ds(pl.multiple_of(k * 256, 256), 256)
            hot = onehot[rows, :]
            want = colb[rows, :]
            total = acc[rows, :]
            for ref, base in refs:
                found = jnp.dot(hot, ref[...], preferred_element_type=F32)
                total = total + jnp.where(want == base, found, 0.0)
            acc[rows, :] = total
            return 0

        lax.fori_loop(0, NG // 256, body, 0)

    for d in (1, 3, 2):
        copies["py", d].wait_recv()
        tile = pall.at[c, lay_of(-d)]
        for e in (1, 3, 2):
            part = tile.at[low]
            copies["a", d, e] = push(("a", d, e), part, part, {"col": col_of(2 * e)})
        copies["sy", d] = push(("sy", d), tile, tile, {"col": sib})
        copies["px", d].wait_recv()
        tile = pall.at[col_of(-2 * d), l]
        for e in (1, 3, 2):
            part = tile.at[high]
            copies["b", d, e] = push(("b", d, e), part, part, {"layer": lay_of(e)})
        copies["sx", d] = push(("sx", d), tile, tile, {"col": sib})
    own_p.wait()

    ring(1)
    pos = lax.broadcasted_iota(jnp.int32, (EX, NG), 0)
    pos = jnp.where(pos < 20, pos, pos - 24).astype(F32)
    expo = g_ref[3:4, :]
    dx = pos - g_ref[5:6, :]
    ex = jnp.where(jnp.abs(dx) <= R, jnp.exp(-expo * dx * dx), 0.0)
    dy = pos - g_ref[6:7, :]
    ey = jnp.where(jnp.abs(dy) <= R, jnp.exp(-expo * dy * dy), 0.0)
    for i in range(EX):
        value = ex[i : i + 1, :] * ey
        upper = value.astype(BF16)
        plane_hi[i * EY : (i + 1) * EY, :] = upper
        plane_lo[i * EY : (i + 1) * EY, :] = (value - upper.astype(F32)).astype(BF16)
    lookup([(c, l)] + [(c, lay_of(-d)) for d in (1, 3, 2)] + [(col_of(-2 * d), l) for d in (1, 3, 2)])
    ring(2)

    copies["ps"].wait_recv()
    for d in (1, 3, 2):
        copies["sy", d].wait_recv()
        copies["sx", d].wait_recv()
    sib_of = lambda d: lax.rem(sib + (d + NC), NC)
    lookup([(sib, l)] + [(sib, lay_of(-d)) for d in (1, 3, 2)] + [(sib_of(-2 * d), l) for d in (1, 3, 2)])
    ring(3)

    for d in (1, 3, 2):
        for e in (1, 3, 2):
            copies["a", d, e].wait_recv()
            part = pall.at[col_of(-2 * e), lay_of(-d), low]
            copies["sa", d, e] = push(("sa", d, e), part, part, {"col": sib})
            copies["b", d, e].wait_recv()
            part = pall.at[col_of(-2 * d), lay_of(-e), high]
            copies["sb", d, e] = push(("sb", d, e), part, part, {"col": sib})
    corners = [(d, e) for d in (1, 3, 2) for e in (1, 3, 2)]
    lookup([(col_of(-2 * d), lay_of(-e)) for d, e in corners])
    ring(4)
    for d, e in corners:
        copies["sa", d, e].wait_recv()
        copies["sb", d, e].wait_recv()
    lookup([(sib_of(-2 * d), lay_of(-e)) for d, e in corners])
    ring(5)

    def deepen(k, _):
        rows = pl.ds(pl.multiple_of(k * 128, 128), 128)
        coef = jnp.sum(acc[rows, :], axis=1, keepdims=True) * gcols[rows, 4:5]
        ez[rows, :] = ez[rows, :] * coef
        return 0

    lax.fori_loop(0, NG // 128, deepen, 0)
    depth = ez[...]
    depth_hi = depth.astype(BF16)
    depth_lo = (depth - depth_hi.astype(F32)).astype(BF16)
    step = 4 * EY
    for k in range(EX // 4):
        rows = slice(k * step, (k + 1) * step)
        part = jnp.dot(plane_hi[rows, :], depth_lo, preferred_element_type=F32)
        part = part + jnp.dot(plane_lo[rows, :], depth_hi, preferred_element_type=F32)
        part = part + jnp.dot(plane_hi[rows, :], depth_hi, preferred_element_type=F32)
        dens[k * 4 : (k + 1) * 4] = part[:, :128].reshape(4, EY, 128)
        gpad[rows, 0:128] = part[:, 128:]
    gpad[EX * EY : 640, 0:128] = jnp.zeros((64, 128), F32)
    for k in range(5):
        turned = jnp.transpose(gpad[k * 128 : (k + 1) * 128, 0:128])
        rim[:, k * 128 : (k + 1) * 128] = turned[0:16, :]
    rim_in[8:120, :] = jnp.zeros((112, 640), F32)
    up = {"layer": lay_of(1)}
    down = {"layer": lay_of(-1)}
    copies["lu"] = push(("lu",), rim.at[0:8], rim_in.at[0:8], up)
    copies["ld"] = push(("ld",), rim.at[8:16], rim_in.at[120:128], down)
    ring(6)

    copies["lu"].wait_recv()
    copies["ld"].wait_recv()
    for k in range(5):
        gpad[k * 128 : (k + 1) * 128, 0:128] = jnp.transpose(rim_in[:, k * 128 : (k + 1) * 128])
    for k in range(EX):
        dens[k] = dens[k] + gpad[k * EY : (k + 1) * EY, 0:128]
    copies["ru"] = push(("ru",), dens.at[16:20], row_in.at[0], right)
    copies["rd"] = push(("rd",), dens.at[20:24], row_in.at[1], left)
    ring(7)

    copies["ru"].wait_recv()
    copies["rd"].wait_recv()
    dens[0:4] = dens[0:4] + row_in[0]
    dens[12:16] = dens[12:16] + row_in[1]
    edge = dens.at[0:16, 16:24]
    copies["cu"] = push(("cu",), edge, col_in.at[0], {"col": col_of(1)})
    copies["cd"] = push(("cd",), edge, col_in.at[1], {"col": col_of(-1)})
    ring(8)

    total = jnp.zeros((256, 128), F32)
    for b in range(NL):
        for k in range(NC // 2):
            lhs = jnp.concatenate([pall[2 * k, b], pall[2 * k + 1, b]], axis=1)
            rhs = hall[b, 4 * k : 4 * k + 4].reshape(256, 128)
            total = total + jnp.dot(lhs, rhs, preferred_element_type=F32)
    prod_ref[...] = total.astype(BF16)

    copies["cu"].wait_recv()
    copies["cd"].wait_recv()
    inner = lax.broadcasted_iota(jnp.int32, (16, 8, 128), 1)
    dens_ref[:, 0:8, :] = dens[0:16, 0:8, :] + jnp.where(inner < 4, col_in[0], 0.0)
    dens_ref[:, 8:16, :] = dens[0:16, 8:16, :] + jnp.where(inner >= 4, col_in[1], 0.0)
    for copy in pending:
        copy.wait_send()


def expand_mask(mask, block):
    return jnp.repeat(jnp.repeat(mask, block, axis=0), block, axis=1) > 0


def on_device(
    p_slabs, p_mask, h_slabs, h_mask, gauss_row, gauss_col, gauss_cell, gauss_expo, gauss_pref
):
    p_local = jnp.where(expand_mask(p_mask[0], BS), p_slabs[0], jnp.zeros_like(p_slabs[0]))
    h_local = jnp.where(expand_mask(h_mask[0], BS), h_slabs[0], jnp.zeros_like(h_slabs[0]))
    h_parts = jnp.transpose(h_local.reshape(64, NL, 128), (1, 0, 2))
    cx = gauss_cell // (GY * GZ)
    cy = gauss_cell // GZ % GY
    cz = gauss_cell % GZ
    gauss = jnp.stack(
        [gauss_row.astype(F32), gauss_col.astype(F32), cz.astype(F32), gauss_expo, gauss_pref,
         cx.astype(F32), cy.astype(F32), jnp.zeros_like(gauss_expo)]
    )
    n_sem = 80
    vmem = pl.BlockSpec(memory_space=pltpu.VMEM)
    return pl.pallas_call(
        kernel,
        out_shape=(
            jax.ShapeDtypeStruct((256, 128), BF16),
            jax.ShapeDtypeStruct((GX, GY, GZ), F32),
        ),
        in_specs=[vmem] * 3,
        out_specs=(vmem, vmem),
        scratch_shapes=[
            pltpu.VMEM((NC, NL, 256, 128), BF16),
            pltpu.VMEM((NL, NR, 64, 128), BF16),
            pltpu.VMEM((640, NG), F32),
            pltpu.VMEM((NG, 128), F32),
            pltpu.VMEM((NG, 256), BF16),
            pltpu.VMEM((NG, 128), F32),
            pltpu.VMEM((NG, 128), F32),
            pltpu.VMEM((NG, 256), F32),
            pltpu.VMEM((EX * EY, NG), BF16),
            pltpu.VMEM((EX * EY, NG), BF16),
            pltpu.VMEM((EX, EY, 128), F32),
            pltpu.VMEM((16, 640), F32),
            pltpu.VMEM((128, 640), F32),
            pltpu.VMEM((2, 4, EY, 128), F32),
            pltpu.VMEM((2, 16, 8, 128), F32),
            pltpu.SemaphoreType.DMA((n_sem,)),
            pltpu.SemaphoreType.DMA((n_sem,)),
            pltpu.SemaphoreType.DMA((2,)),
        ],
        compiler_params=pltpu.CompilerParams(collective_id=0, has_side_effects=True),
    )(p_local, h_parts, gauss)


def solution(mesh):
    placed = (
        P("layer", "row", "col"),
        P("layer", "row", "col"),
        P("layer", "row", "col"),
        P("layer", "row", "col"),
        P(("row", "col", "layer")),
        P(("row", "col", "layer")),
        P(("row", "col", "layer")),
        P(("row", "col", "layer")),
        P(("row", "col", "layer")),
    )
    return jax.shard_map(
        on_device,
        mesh=mesh,
        in_specs=placed,
        out_specs=(P("row", ("col", "layer")), P("row", "col", "layer")),
        check_vma=False,
    )
```

time: 189 us -> 64.1 us (0.34)
  waiting for transfers between devices: 100 us -> 0 us
  Pallas kernels: 0 us -> 52.8 us
  starting transfers between devices: 21.7 us -> 0 us
  blocking collectives: 19.6 us -> 0 us
  between operations: 14.3 us -> 0.74 us
  local copies, waits for them, and re-layouts: 21 us -> 8.78 us
  other arithmetic: 6.68 us -> 1.32 us
  matrix products: 4.1 us -> 0 us
    all_gather x2 -> x0, waiting for transfers between devices: 83.7 us -> none  [the longest x1 42.3 us: on_device(): h_slab = lax.all_gather(h_eff, 'row', axis=0, tiled=True)]
    pallas_call x0 -> x1, Pallas kernels: none -> 52.8 us  [on_device(): pl.pallas_call(kernel, out_shape=(jax.ShapeDtypeStruct((256, 128), BF16),...]
    all_gather x1 -> x0, blocking collectives: 19.6 us -> none  [on_device(): p_whole = lax.all_gather(p_local, 'col', axis=1, tiled=True)]
    ppermute x6 -> x0, starting transfers between devices: 17.4 us -> none  [the longest x3 9.99 us: with_halo(): lax.ppermute(lax.slice_in_dim(block, 0, width, axis=dim), axis, backward)]
    ppermute x6 -> x0, waiting for transfers between devices: 16.6 us -> none  [the longest x3 13.2 us: with_halo(): lax.ppermute(lax.slice_in_dim(block, block.shape[dim] - width, None, axis...]
    gather x1 -> x0, local copies, waits for them, and re-layouts: 13.1 us -> none  [on_device(): coef = gauss_pref * p_rows[gauss_row, gauss_col].astype(jnp.float32)]
    unnamed x11 -> x22, local copies, waits for them, and re-layouts: 1.95 us -> 7.38 us
    all_to_all x1 -> x0, starting transfers between devices: 4.13 us -> none  [on_device(): lax.all_to_all(h_slab, 'layer', split_axis=1, concat_axis=0, tiled=True)]
  transfers between devices with their start and end apart: 9 -> 0, of which waited for: 7 -> 0; matrix products, arithmetic and copies ran while one was open for 14% -> 0% of each run, Pallas kernels for 0% -> 0%
where the time goes in v1:
time: 64.1 us; the launch traced here: 63.6 us
  Pallas kernels  52.8 us (82%)
  local copies, waits for them, and re-layouts  8.78 us (14%)
  other arithmetic  1.32 us (2%)
  between operations  0.74 us (1%)
    pallas_call x1, Pallas kernels, on_device(): pl.pallas_call(kernel, out_shape=(jax.ShapeDtypeStruct((256, 128), BF16),...  52.8 us
    unnamed x22, local copies, waits for them, and re-layouts  7.38 us

profile of v1, /device:TPU:1, one launch (start us, length us, event | category | flops | bytes accessed | tf_op | source)
XLA Modules:
  0.0 63.6 jit_solution(15979259881961034303)
XLA Ops:
  0.6 0.0 copy-start.8
  0.6 0.7 %copy-done.8 = s32[1,8,4]{1,2,0:T(4,128)S(1)} copy-done((s32[1,8,4]{1,2,0:T(4,128)S(1)}, s32[1,8,4]{1,2,0:T(4,128)}, u32[]{:S(2)}) %copy-start.8) | copy-done | bytes 152
  1.3 0.0 copy-start.9
  1.3 0.7 %copy-done.9 = s32[1,2,16]{2,1,0:T(2,128)S(1)} copy-done((s32[1,2,16]{2,1,0:T(2,128)S(1)}, s32[1,2,16]{2,1,0:T(2,128)}, u32[]{:S(2)}) %copy-start.9) | copy-done | bytes 152
  2.0 0.1 copy.17
  2.1 0.0 copy-start.5
  2.1 0.1 broadcast_in_dim.18
  2.2 0.1 gt.38
  2.3 0.5 copy-done.5
  2.8 0.0 copy-start.6
  2.8 0.7 %copy-done.6 = s32[1024]{0:T(1024)S(1)} copy-done((s32[1024]{0:T(1024)S(1)}, s32[1024]{0:T(1024)}, u32[]{:S(2)}) %copy-start.6) | copy-done | bytes 4120
  3.5 0.1 broadcast_in_dim.21
  3.6 0.0 copy-start.7
  3.6 0.1 gt.43
  3.7 0.6 copy-done.7
  4.3 0.0 copy-start.3
  4.3 0.0 copy-start.4
  4.3 0.7 %copy-done.3 = f32[1024]{0:T(1024)S(1)} copy-done((f32[1024]{0:T(1024)S(1)}, f32[1024]{0:T(1024)}, u32[]{:S(2)}) %copy-start.3) | copy-done | bytes 4120
  5.0 0.0 copy-done.4
  5.0 0.7 %stack.31.g_ref = f32[8,1024]{1,0:T(8,128)} concatenate(f32[1,1024]{1,0:T(1,128)S(1)} %bitcast.23, f32[1,1024]{1,0:T(1,128)S(1)} %bitcast.24, f32[1,1024]{1,0:T(1,128)S(1)} %bitcast.27, f32[1,1024]{1,0:T(1,128)S(1)} %bitcast.28, f32[1,1024]{1,0:T(1,128)S(1)} %bitcast.29, f32[1,1024]{1,0:T(1,128)S(1)} %bitcast.26, f32[1,1024]{1,0:T(1,128)S(1)} %bitcast.25, ...), dimensions={0} | concatenate | bytes 65536 | tf_op jit(solution)/shard_map/stack | solution.py:265
  5.6 0.0 copy-start.1
  5.7 0.1 copy.16
  5.8 0.7 %copy-done.1 = bf16[1,256,128]{2,1,0:T(8,128)(2,1)S(1)} copy-done((bf16[1,256,128]{2,1,0:T(8,128)(2,1)S(1)}, bf16[1,256,128]{2,1,0:T(8,128)(2,1)}, u32[]{:S(2)}) %copy-start.1) | copy-done | bytes 65560
  6.5 0.6 %bitcast_select_fusion.p_ref = bf16[256,128]{1,0:T(8,128)(2,1)} fusion(pred[256,128]{1,0:T(8,128)(4,1)S(1)} %copy.16, bf16[1,256,128]{2,1,0:T(8,128)(2,1)S(1)} %copy-done.1), kind=kLoop, calls=%fused_computation | loop fusion | flops 32768 | bytes 163840 | tf_op jit(solution)/shard_map/jit(_where)/select_n | solution.py:259
  7.1 0.0 copy-start.2
  7.1 0.1 copy.18
  7.3 0.7 %copy-done.2 = bf16[1,64,512]{2,1,0:T(8,128)(2,1)S(1)} copy-done((bf16[1,64,512]{2,1,0:T(8,128)(2,1)S(1)}, bf16[1,64,512]{2,1,0:T(8,128)(2,1)}, u32[]{:S(2)}) %copy-start.2) | copy-done | bytes 65560
  8.0 0.6 %fusion.h_ref = bf16[4,64,128]{2,1,0:T(8,128)(2,1)} fusion(pred[64,4,128]{2,0,1:T(8,128)(4,1)S(1)} %copy.18, bf16[64,4,128]{2,1,0:T(4,128)(2,1)S(1)} %squeeze.9), kind=kLoop, calls=%fused_computation.2 | loop fusion | flops 32768 | bytes 163840 | tf_op jit(solution)/shard_map/transpose | solution.py:261
  8.6 52.8 %shard_map.104 = (bf16[256,128]{1,0:T(8,128)(2,1)}, f32[16,16,128]{2,1,0:T(8,128)}) custom-call(bf16[256,128]{1,0:T(8,128)(2,1)} %bitcast_select_fusion.p_ref, bf16[4,64,128]{2,1,0:T(8,128)(2,1)} %fusion.h_ref, f32[8,1024]{1,0:T(8,128)} %stack.31.g_ref), custom_call_target="tpu_custom_call" | custom-call | tf_op jit(solution)/shard_map/pallas_call | solution.py:271
  61.5 0.0 copy-start
  61.5 1.5 %copy.25 = bf16[256,128]{1,0:T(8,128)(2,1)} copy(bf16[256,128]{1,0:T(8,128)(2,1)} %get-tuple-element.7) | data formatting | bytes 131072
  63.0 0.0 copy-done
  63.0 0.7 %copy.26 = f32[16,16,128]{2,1,0:T(8,128)} copy(f32[16,16,128]{2,1,0:T(8,128)S(1)} %copy-done) | data formatting | bytes 262144
  (9 shorter events, 0.1 us)
Async XLA Ops:
  0.6 0.7 %copy-start.8 = (s32[1,8,4]{1,2,0:T(4,128)S(1)}, s32[1,8,4]{1,2,0:T(4,128)}, u32[]{:S(2)}) copy-start(s32[1,8,4]{1,2,0:T(4,128)} %param.10) | copy-start | bytes 388
  1.3 0.7 %copy-start.9 = (s32[1,2,16]{2,1,0:T(2,128)S(1)}, s32[1,2,16]{2,1,0:T(2,128)}, u32[]{:S(2)}) copy-start(s32[1,2,16]{2,1,0:T(2,128)} %param.12) | copy-start | bytes 388
  2.1 0.7 %copy-start.5 = (s32[1024]{0:T(1024)S(1)}, s32[1024]{0:T(1024)}, u32[]{:S(2)}) copy-start(s32[1024]{0:T(1024)} %param.13) | copy-start | bytes 12292
  2.8 0.7 %copy-start.6 = (s32[1024]{0:T(1024)S(1)}, s32[1024]{0:T(1024)}, u32[]{:S(2)}) copy-start(s32[1024]{0:T(1024)} %param.14) | copy-start | bytes 12292
  3.6 0.7 %copy-start.7 = (s32[1024]{0:T(1024)S(1)}, s32[1024]{0:T(1024)}, u32[]{:S(2)}) copy-start(s32[1024]{0:T(1024)} %param.15) | copy-start | bytes 12292
  4.3 0.7 %copy-start.3 = (f32[1024]{0:T(1024)S(1)}, f32[1024]{0:T(1024)}, u32[]{:S(2)}) copy-start(f32[1024]{0:T(1024)} %param.16) | copy-start | bytes 12292
  4.3 0.7 %copy-start.4 = (f32[1024]{0:T(1024)S(1)}, f32[1024]{0:T(1024)}, u32[]{:S(2)}) copy-start(f32[1024]{0:T(1024)} %param.17) | copy-start | bytes 12292
  5.6 0.8 %copy-start.1 = (bf16[1,256,128]{2,1,0:T(8,128)(2,1)S(1)}, bf16[1,256,128]{2,1,0:T(8,128)(2,1)}, u32[]{:S(2)}) copy-start(bf16[1,256,128]{2,1,0:T(8,128)(2,1)} %param.9) | copy-start | bytes 196612
  7.1 0.8 %copy-start.2 = (bf16[1,64,512]{2,1,0:T(8,128)(2,1)S(1)}, bf16[1,64,512]{2,1,0:T(8,128)(2,1)}, u32[]{:S(2)}) copy-start(bf16[1,64,512]{2,1,0:T(8,128)(2,1)} %param.11) | copy-start | bytes 196612
  61.5 1.5 %copy-start = (f32[16,16,128]{2,1,0:T(8,128)S(1)}, f32[16,16,128]{2,1,0:T(8,128)}, u32[]{:S(2)}) copy-start(f32[16,16,128]{2,1,0:T(8,128)} %get-tuple-element.8) | copy-start | bytes 393220

commit v2 on v1

v2 whole, which is shorter than its diff:
```python
import jax
import jax.numpy as jnp
from jax import lax
from jax.experimental import pallas as pl
from jax.experimental.pallas import tpu as pltpu
from jax.sharding import PartitionSpec as P

BS = 32
GX = 16
GY = 16
GZ = 128
R = 4
NG = 1024
NR = 16
NC = 8
NL = 4
EX = GX + 2 * R
EY = GY + 2 * R
F32 = jnp.float32
BF16 = jnp.bfloat16


def kernel(
    p_hbm, pm_hbm, h_hbm, hm_hbm, row_hbm, gcol_hbm, cell_hbm, expo_hbm, pref_hbm, prod_ref, dens_ref,
    p_in, pm_in, h_in, hm_in, g_int, g_float, h_ref, turn, pall, hall, gpad, gcols, onehot, colb, acc, ez, plane_hi, plane_lo, dens, rim, rim_in, row_in, col_in,
    send, recv, local,
):
    r = lax.axis_index("row")
    c = lax.axis_index("col")
    l = lax.axis_index("layer")
    row_of = lambda d: lax.rem(r + (d + NR), NR)
    col_of = lambda d: lax.rem(c + (d + NC), NC)
    lay_of = lambda d: lax.rem(l + (d + NL), NL)
    odd = lax.rem(c, 2)
    sib = c + 1 - 2 * odd
    out = c - 1 + 2 * odd
    other = lax.rem(out + NC, NC)

    loads = [
        pltpu.make_async_copy(src, dst, local.at[2 + n])
        for n, (src, dst) in enumerate(
            [(p_hbm, p_in), (pm_hbm, pm_in), (h_hbm, h_in), (hm_hbm, hm_in), (row_hbm, g_int.at[0]), (gcol_hbm, g_int.at[1]),
             (cell_hbm, g_int.at[2]), (expo_hbm, g_float.at[0]), (pref_hbm, g_float.at[1])]
        )
    ]
    for copy in loads:
        copy.start()
    barrier = pltpu.get_barrier_semaphore()
    peers = (
        [{"layer": lay_of(d)} for d in (1, 2, 3)]
        + [{"col": col_of(2 * d)} for d in (1, 2, 3)]
        + [{"col": sib}, {"col": other}, {"row": row_of(1)}, {"row": row_of(-1)}]
    )
    for peer in peers:
        pl.semaphore_signal(barrier, inc=1, device_id=peer, device_id_type=pl.DeviceIdType.MESH)
    block = lax.broadcasted_iota(jnp.int32, (4, 128), 0)
    of_lane = lax.broadcasted_iota(jnp.int32, (4, 128), 1) // BS
    loads[0].wait()
    loads[1].wait()
    for i in range(256 // BS):
        column = jnp.broadcast_to(pm_in[:, i : i + 1], (4, 128))
        keep = jnp.sum(jnp.where(block == of_lane, column, 0), axis=0, keepdims=True) > 0
        rows = slice(i * BS, (i + 1) * BS)
        value = jnp.where(jnp.broadcast_to(keep, (BS, 128)), p_in[rows, :].astype(F32), 0.0)
        pall[c, l, rows, :] = value.astype(BF16)
    loads[2].wait()
    loads[3].wait()
    of_lane = lax.broadcasted_iota(jnp.int32, (1, 128), 1) // BS
    for q in range(NL):
        for i in range(64 // BS):
            keep = jnp.zeros((1, 128), jnp.int32)
            for j in range(4):
                at = q * 4 + j
                keep = jnp.where(of_lane == j, jnp.broadcast_to(hm_in[i : i + 1, at : at + 1], (1, 128)), keep)
            rows = slice(i * BS, (i + 1) * BS)
            value = h_in[rows, q * 128 : (q + 1) * 128].astype(F32)
            value = jnp.where(jnp.broadcast_to(keep > 0, (BS, 128)), value, 0.0)
            h_ref[q, rows, :] = value.astype(BF16)
    own_h = pltpu.make_async_copy(h_ref.at[l], hall.at[l, r], local.at[1])
    own_h.start()
    p_ref = pall.at[c, l]
    pl.semaphore_wait(barrier, len(peers))

    pending = []
    slots = {}

    def push(key, src, dst, peer):
        n = slots.setdefault(key, len(slots))
        copy = pltpu.make_async_remote_copy(
            src_ref=src, dst_ref=dst, send_sem=send.at[n], recv_sem=recv.at[n],
            device_id=peer, device_id_type=pl.DeviceIdType.MESH,
        )
        copy.start()
        pending.append(copy)
        return copy

    low = pl.ds(0, 128)
    high = pl.ds(128, 128)
    copies = {}
    right = {"row": row_of(1)}
    left = {"row": row_of(-1)}
    order = (0, 1, 3, 2)
    last = NR // 2 - 1
    for d in (1, 3, 2):
        copies["ha", d] = push(("ha", d), h_ref.at[lay_of(d)], hall.at[l, r], {"layer": lay_of(d)})
    own_h.wait()
    piece = hall.at[l, r]
    copies["hr", 0, 0] = push(("hr", 0, 0), piece, piece, right)
    copies["hl", 0, 0] = push(("hl", 0, 0), piece, piece, left)
    for d in (1, 3, 2):
        copies["py", d] = push(("py", d), p_ref, pall.at[c, l], {"layer": lay_of(d)})
        copies["px", d] = push(("px", d), p_ref, pall.at[c, l], {"col": col_of(2 * d)})
    copies["ps"] = push(("ps",), p_ref, pall.at[c, l], {"col": sib})

    for copy in loads[4:]:
        copy.wait()
    cell = g_int[2]
    turn[0:8, :] = g_int[0].astype(F32)
    turn[8:16, :] = g_int[1].astype(F32)
    turn[16:24, :] = (cell & (GZ - 1)).astype(F32)
    turn[24:32, :] = g_float[0]
    turn[32:40, :] = g_float[1]
    turn[40:128, :] = jnp.zeros((88, 128), F32)
    gcols[...] = jnp.transpose(turn[...])

    def ring_start():
        for d in order[1:]:
            copies["ha", d].wait_recv()
            piece = hall.at[lay_of(-d), r]
            copies["hr", 0, d] = push(("hr", 0, d), piece, piece, right)
            copies["hl", 0, d] = push(("hl", 0, d), piece, piece, left)

    def ring(s):
        for d in order:
            for way, sign, peer, extra in (("hr", -1, right, (0, 1)), ("hl", 1, left, (3, 2))):
                if (way, s - 1, d) in copies:
                    copies[way, s - 1, d].wait_recv()
                    if s < last or (s == last and d in extra):
                        piece = hall.at[lay_of(-d), row_of(sign * s)]
                        copies[way, s, d] = push((way, s, d), piece, piece, peer)

    ring_start()
    lane = lax.broadcasted_iota(jnp.int32, (128, 256), 1)
    lane_f = lane.astype(F32)
    pos_z = jnp.where(lane < 136, lane, lane - 144).astype(F32)
    near_z = (lane < 132) | ((lane >= 140) & (lane < 144))
    for k in range(NG // 128):
        rows = slice(k * 128, (k + 1) * 128)
        onehot[rows, :] = jnp.where(gcols[:, k : k + 1] == lane_f, 1.0, 0.0).astype(BF16)
        colb[rows, :] = gcols[:, 8 + k : 9 + k] - lane_f[:, :128]
        acc[rows, :] = jnp.zeros((128, 128), F32)

    def lookup(tiles):
        refs = [(pall.at[a, b], (b * NG + a * 128).astype(F32)) for a, b in tiles]

        def body(k, _):
            rows = pl.ds(pl.multiple_of(k * 256, 256), 256)
            hot = onehot[rows, :]
            want = colb[rows, :]
            total = acc[rows, :]
            for ref, base in refs:
                found = jnp.dot(hot, ref[...], preferred_element_type=F32)
                total = total + jnp.where(want == base, found, 0.0)
            acc[rows, :] = total
            return 0

        lax.fori_loop(0, NG // 256, body, 0)

    for d in (1, 3, 2):
        copies["py", d].wait_recv()
        tile = pall.at[c, lay_of(-d)]
        for e in (1, 3, 2):
            part = tile.at[low]
            copies["a", d, e] = push(("a", d, e), part, part, {"col": col_of(2 * e)})
        copies["sy", d] = push(("sy", d), tile, tile, {"col": sib})
        copies["px", d].wait_recv()
        tile = pall.at[col_of(-2 * d), l]
        for e in (1, 3, 2):
            part = tile.at[high]
            copies["b", d, e] = push(("b", d, e), part, part, {"layer": lay_of(e)})
        copies["sx", d] = push(("sx", d), tile, tile, {"col": sib})

    ring(1)
    pos = lax.broadcasted_iota(jnp.int32, (EX, 128), 0)
    pos = jnp.where(pos < 20, pos, pos - 24).astype(F32)
    for k in range(NG // 128):
        rows = slice(k * 128, (k + 1) * 128)
        dz = pos_z - gcols[:, 16 + k : 17 + k]
        value = jnp.exp(-gcols[:, 24 + k : 25 + k] * dz * dz)
        ez[rows, :] = jnp.where(near_z & (jnp.abs(dz) <= R), value, 0.0)

    def make_plane(k, _):
        cols = pl.ds(pl.multiple_of(k * 128, 128), 128)
        at = g_int[2, pl.ds(k, 1), :]
        expo = g_float[0, pl.ds(k, 1), :]
        dx = pos - (at >> 11).astype(F32)
        ex = jnp.where(jnp.abs(dx) <= R, jnp.exp(-expo * dx * dx), 0.0)
        dy = pos - ((at >> 7) & (GY - 1)).astype(F32)
        ey = jnp.where(jnp.abs(dy) <= R, jnp.exp(-expo * dy * dy), 0.0)
        for i in range(0, EX, 2):
            value = jnp.concatenate([ex[i : i + 1, :] * ey, ex[i + 1 : i + 2, :] * ey], axis=0)
            upper = value.astype(BF16)
            plane_hi[i * EY : (i + 2) * EY, cols] = upper
            plane_lo[i * EY : (i + 2) * EY, cols] = (value - upper.astype(F32)).astype(BF16)
        return 0

    lax.fori_loop(0, NG // 128, make_plane, 0)
    lookup([(c, l)] + [(c, lay_of(-d)) for d in (1, 3, 2)] + [(col_of(-2 * d), l) for d in (1, 3, 2)])
    ring(2)

    copies["ps"].wait_recv()
    for d in (1, 3, 2):
        copies["sy", d].wait_recv()
        copies["sx", d].wait_recv()
    sib_of = lambda d: lax.rem(sib + (d + NC), NC)
    lookup([(sib, l)] + [(sib, lay_of(-d)) for d in (1, 3, 2)] + [(sib_of(-2 * d), l) for d in (1, 3, 2)])

    for d in (1, 3, 2):
        for e in (1, 3, 2):
            copies["a", d, e].wait_recv()
            part = pall.at[col_of(-2 * e), lay_of(-d), low]
            copies["sa", d, e] = push(("sa", d, e), part, part, {"col": sib})
            copies["b", d, e].wait_recv()
            part = pall.at[col_of(-2 * d), lay_of(-e), high]
            copies["sb", d, e] = push(("sb", d, e), part, part, {"col": sib})
    corners = [(d, e) for d in (1, 3, 2) for e in (1, 3, 2)]
    lookup([(col_of(-2 * d), lay_of(-e)) for d, e in corners])
    ring(3)
    for d, e in corners:
        copies["sa", d, e].wait_recv()
        copies["sb", d, e].wait_recv()
    lookup([(sib_of(-2 * d), lay_of(-e)) for d, e in corners])

    for k in range(NG // 128):
        rows = slice(k * 128, (k + 1) * 128)
        coef = jnp.sum(acc[rows, :], axis=1, keepdims=True) * gcols[:, 32 + k : 33 + k]
        ez[rows, :] = ez[rows, :] * coef

    depth = ez[...]
    depth_hi = depth.astype(BF16)
    depth_lo = (depth - depth_hi.astype(F32)).astype(BF16)
    step = 4 * EY
    for k in range(EX // 4):
        rows = slice(k * step, (k + 1) * step)
        part = jnp.dot(plane_hi[rows, :], depth_lo, preferred_element_type=F32)
        part = part + jnp.dot(plane_lo[rows, :], depth_hi, preferred_element_type=F32)
        part = part + jnp.dot(plane_hi[rows, :], depth_hi, preferred_element_type=F32)
        dens[k * 4 : (k + 1) * 4] = part[:, :128].reshape(4, EY, 128)
        gpad[rows, :] = part[:, 128:]
    gpad[EX * EY : 640, :] = jnp.zeros((64, 128), F32)
    for k in range(5):
        turned = jnp.transpose(gpad[k * 128 : (k + 1) * 128, :])
        rim[:, k * 128 : (k + 1) * 128] = turned[0:16, :]
    rim_in[8:120, :] = jnp.zeros((112, 640), F32)
    up = {"layer": lay_of(1)}
    down = {"layer": lay_of(-1)}
    copies["lu"] = push(("lu",), rim.at[0:8], rim_in.at[0:8], up)
    copies["ld"] = push(("ld",), rim.at[8:16], rim_in.at[120:128], down)
    ring(4)
    ring(5)

    copies["lu"].wait_recv()
    copies["ld"].wait_recv()
    for k in range(5):
        gpad[k * 128 : (k + 1) * 128, :] = jnp.transpose(rim_in[:, k * 128 : (k + 1) * 128])
    for k in range(EX):
        dens[k] = dens[k] + gpad[k * EY : (k + 1) * EY, :]
    copies["ru"] = push(("ru",), dens.at[16:20], row_in.at[0], right)
    copies["rd"] = push(("rd",), dens.at[20:24], row_in.at[1], left)
    ring(6)

    copies["ru"].wait_recv()
    copies["rd"].wait_recv()
    dens[0:4] = dens[0:4] + row_in[0]
    dens[12:16] = dens[12:16] + row_in[1]
    edge = dens.at[0:16, 16:24]
    copies["cu"] = push(("cu",), edge, col_in.at[0], {"col": col_of(1)})
    copies["cd"] = push(("cd",), edge, col_in.at[1], {"col": col_of(-1)})
    ring(7)
    ring(8)

    total = jnp.zeros((256, 128), F32)
    for b in range(NL):
        for k in range(NC // 2):
            lhs = jnp.concatenate([pall[2 * k, b], pall[2 * k + 1, b]], axis=1)
            rhs = hall[b, 4 * k : 4 * k + 4].reshape(256, 128)
            total = total + jnp.dot(lhs, rhs, preferred_element_type=F32)
    prod_ref[...] = total.astype(BF16)

    copies["cu"].wait_recv()
    copies["cd"].wait_recv()
    inner = lax.broadcasted_iota(jnp.int32, (16, 8, 128), 1)
    dens_ref[:, 0:8, :] = dens[0:16, 0:8, :] + jnp.where(inner < 4, col_in[0], 0.0)
    dens_ref[:, 8:16, :] = dens[0:16, 8:16, :] + jnp.where(inner >= 4, col_in[1], 0.0)
    for copy in pending:
        copy.wait_send()


def on_device(
    p_slabs, p_mask, h_slabs, h_mask, gauss_row, gauss_col, gauss_cell, gauss_expo, gauss_pref
):
    n_sem = 128
    vmem = pl.BlockSpec(memory_space=pltpu.VMEM)
    return pl.pallas_call(
        kernel,
        out_shape=(
            jax.ShapeDtypeStruct((256, 128), BF16),
            jax.ShapeDtypeStruct((GX, GY, GZ), F32),
        ),
        in_specs=[pl.BlockSpec(memory_space=pl.ANY)] * 9,
        out_specs=(vmem, vmem),
        scratch_shapes=[
            pltpu.VMEM((256, 128), BF16),
            pltpu.VMEM((4, 8), jnp.int32),
            pltpu.VMEM((64, 512), BF16),
            pltpu.VMEM((2, 16), jnp.int32),
            pltpu.VMEM((3, 8, 128), jnp.int32),
            pltpu.VMEM((2, 8, 128), F32),
            pltpu.VMEM((NL, 64, 128), BF16),
            pltpu.VMEM((128, 128), F32),
            pltpu.VMEM((NC, NL, 256, 128), BF16),
            pltpu.VMEM((NL, NR, 64, 128), BF16),
            pltpu.VMEM((640, 128), F32),
            pltpu.VMEM((128, 128), F32),
            pltpu.VMEM((NG, 256), BF16),
            pltpu.VMEM((NG, 128), F32),
            pltpu.VMEM((NG, 128), F32),
            pltpu.VMEM((NG, 256), F32),
            pltpu.VMEM((EX * EY, NG), BF16),
            pltpu.VMEM((EX * EY, NG), BF16),
            pltpu.VMEM((EX, EY, 128), F32),
            pltpu.VMEM((16, 640), F32),
            pltpu.VMEM((128, 640), F32),
            pltpu.VMEM((2, 4, EY, 128), F32),
            pltpu.VMEM((2, 16, 8, 128), F32),
            pltpu.SemaphoreType.DMA((n_sem,)),
            pltpu.SemaphoreType.DMA((n_sem,)),
            pltpu.SemaphoreType.DMA((11,)),
        ],
        compiler_params=pltpu.CompilerParams(collective_id=0, has_side_effects=True),
    )(
        p_slabs[0], jnp.transpose(p_mask[0]), h_slabs[0], h_mask[0],
        gauss_row.reshape(8, 128), gauss_col.reshape(8, 128), gauss_cell.reshape(8, 128),
        gauss_expo.reshape(8, 128), gauss_pref.reshape(8, 128),
    )


def solution(mesh):
    placed = (
        P("layer", "row", "col"),
        P("layer", "row", "col"),
        P("layer", "row", "col"),
        P("layer", "row", "col"),
        P(("row", "col", "layer")),
        P(("row", "col", "layer")),
        P(("row", "col", "layer")),
        P(("row", "col", "layer")),
        P(("row", "col", "layer")),
    )
    return jax.shard_map(
        on_device,
        mesh=mesh,
        in_specs=placed,
        out_specs=(P("row", ("col", "layer")), P("row", "col", "layer")),
        check_vma=False,
    )
```

time: 64.1 us -> 50.6 us (0.79)
  the two profiles are of different devices: /device:TPU:1 before, /device:TPU:32 now
where the time goes in v2:
time: 50.6 us; the launch traced here: 50.4 us
  Pallas kernels  47.6 us (94%)
  local copies, waits for them, and re-layouts  2.17 us (4%)
  between operations  0.65 us (1%)
    pallas_call x1, Pallas kernels, on_device(): pl.pallas_call(kernel, out_shape=(jax.ShapeDtypeStruct((256, 128), BF16),...  47.6 us
    unnamed x4, local copies, waits for them, and re-layouts  2.17 us

profile of v2, /device:TPU:32, one launch (start us, length us, event | category | flops | bytes accessed | tf_op | source)
XLA Modules:
  0.0 50.4 jit_solution(1916247828977405691)
XLA Ops:
  0.6 47.6 %shard_map.104 = (bf16[256,128]{1,0:T(8,128)(2,1)}, f32[16,16,128]{2,1,0:T(8,128)}) custom-call(bf16[256,128]{1,0:T(8,128)(2,1)} %bitcast.11, s32[4,8]{1,0:T(4,128)} %bitcast.18, bf16[64,512]{1,0:T(8,128)(2,1)} %bitcast.12, s32[2,16]{1,0:T(2,128)} %bitcast.19, s32[8,128]{1,0:T(8,128)} %bitcast.13, s32[8,128]{1,0:T(8,128)} %bitcast.14, s32[8,128]{1,0:T(8,128)} %bitcast.15, ...), custom_call_target="tpu_custom_call" | custom-call | tf_op jit(solution)/shard_map/pallas_call | solution.py:304
  48.2 0.0 copy-start
  48.2 1.5 %copy.13 = bf16[256,128]{1,0:T(8,128)(2,1)} copy(bf16[256,128]{1,0:T(8,128)(2,1)} %get-tuple-element.4) | data formatting | bytes 131072
  49.7 0.0 copy-done
  49.7 0.7 %copy.14 = f32[16,16,128]{2,1,0:T(8,128)} copy(f32[16,16,128]{2,1,0:T(8,128)S(1)} %copy-done) | data formatting | bytes 262144
Async XLA Ops:
  48.2 1.5 %copy-start = (f32[16,16,128]{2,1,0:T(8,128)S(1)}, f32[16,16,128]{2,1,0:T(8,128)}, u32[]{:S(2)}) copy-start(f32[16,16,128]{2,1,0:T(8,128)} %get-tuple-element.5) | copy-start | bytes 393220

commit v3 on v2

--- a/solution.py
+++ b/solution.py
@@ -49,7 +49,8 @@
     peers = (
         [{"layer": lay_of(d)} for d in (1, 2, 3)]
         + [{"col": col_of(2 * d)} for d in (1, 2, 3)]
-        + [{"col": sib}, {"col": other}, {"row": row_of(1)}, {"row": row_of(-1)}]
+        + [{"col": sib}, {"col": other}]
+        + [{"row": row_of(d)} for d in (1, -1, 2, -2)]
     )
     for peer in peers:
         pl.semaphore_signal(barrier, inc=1, device_id=peer, device_id_type=pl.DeviceIdType.MESH)
@@ -100,13 +101,29 @@
     right = {"row": row_of(1)}
     left = {"row": row_of(-1)}
     order = (0, 1, 3, 2)
-    last = NR // 2 - 1
+    tree = [
+        (0, 2), (0, -2), (0, 1), (0, -1), (2, 4), (-2, -4), (2, 3), (-2, -3),
+        (4, 6), (-4, -6), (4, 5), (-4, -5), (6, 8), (6, 7), (-6, -7),
+    ]
+
+    def spread(parent, d):
+        if parent:
+            copies["h", parent, d].wait_recv()
+        for source, target in tree:
+            if source == parent:
+                piece = hall.at[lay_of(-d), row_of(-parent)]
+                peer = {"row": row_of(target - parent)}
+                copies["h", target, d] = push(("h", target, d), piece, piece, peer)
+
+    def hop(parent):
+        for d in order:
+            spread(parent, d)
+            spread(-parent, d)
+
     for d in (1, 3, 2):
         copies["ha", d] = push(("ha", d), h_ref.at[lay_of(d)], hall.at[l, r], {"layer": lay_of(d)})
     own_h.wait()
-    piece = hall.at[l, r]
-    copies["hr", 0, 0] = push(("hr", 0, 0), piece, piece, right)
-    copies["hl", 0, 0] = push(("hl", 0, 0), piece, piece, left)
+    spread(0, 0)
     for d in (1, 3, 2):
         copies["py", d] = push(("py", d), p_ref, pall.at[c, l], {"layer": lay_of(d)})
         copies["px", d] = push(("px", d), p_ref, pall.at[c, l], {"col": col_of(2 * d)})
@@ -123,23 +140,9 @@
     turn[40:128, :] = jnp.zeros((88, 128), F32)
     gcols[...] = jnp.transpose(turn[...])
 
-    def ring_start():
-        for d in order[1:]:
-            copies["ha", d].wait_recv()
-            piece = hall.at[lay_of(-d), r]
-            copies["hr", 0, d] = push(("hr", 0, d), piece, piece, right)
-            copies["hl", 0, d] = push(("hl", 0, d), piece, piece, left)
-
-    def ring(s):
-        for d in order:
-            for way, sign, peer, extra in (("hr", -1, right, (0, 1)), ("hl", 1, left, (3, 2))):
-                if (way, s - 1, d) in copies:
-                    copies[way, s - 1, d].wait_recv()
-                    if s < last or (s == last and d in extra):
-                        piece = hall.at[lay_of(-d), row_of(sign * s)]
-                        copies[way, s, d] = push((way, s, d), piece, piece, peer)
-
-    ring_start()
+    for d in order[1:]:
+        copies["ha", d].wait_recv()
+        spread(0, d)
     lane = lax.broadcasted_iota(jnp.int32, (128, 256), 1)
     lane_f = lane.astype(F32)
     pos_z = jnp.where(lane < 136, lane, lane - 144).astype(F32)
@@ -180,7 +183,6 @@
             copies["b", d, e] = push(("b", d, e), part, part, {"layer": lay_of(e)})
         copies["sx", d] = push(("sx", d), tile, tile, {"col": sib})
 
-    ring(1)
     pos = lax.broadcasted_iota(jnp.int32, (EX, 128), 0)
     pos = jnp.where(pos < 20, pos, pos - 24).astype(F32)
     for k in range(NG // 128):
@@ -206,7 +208,7 @@
 
     lax.fori_loop(0, NG // 128, make_plane, 0)
     lookup([(c, l)] + [(c, lay_of(-d)) for d in (1, 3, 2)] + [(col_of(-2 * d), l) for d in (1, 3, 2)])
-    ring(2)
+    hop(2)
 
     copies["ps"].wait_recv()
     for d in (1, 3, 2):
@@ -225,7 +227,7 @@
             copies["sb", d, e] = push(("sb", d, e), part, part, {"col": sib})
     corners = [(d, e) for d in (1, 3, 2) for e in (1, 3, 2)]
     lookup([(col_of(-2 * d), lay_of(-e)) for d, e in corners])
-    ring(3)
+    hop(4)
     for d, e in corners:
         copies["sa", d, e].wait_recv()
         copies["sb", d, e].wait_recv()
@@ -256,8 +258,6 @@
     down = {"layer": lay_of(-1)}
     copies["lu"] = push(("lu",), rim.at[0:8], rim_in.at[0:8], up)
     copies["ld"] = push(("ld",), rim.at[8:16], rim_in.at[120:128], down)
-    ring(4)
-    ring(5)
 
     copies["lu"].wait_recv()
     copies["ld"].wait_recv()
@@ -267,7 +267,7 @@
         dens[k] = dens[k] + gpad[k * EY : (k + 1) * EY, :]
     copies["ru"] = push(("ru",), dens.at[16:20], row_in.at[0], right)
     copies["rd"] = push(("rd",), dens.at[20:24], row_in.at[1], left)
-    ring(6)
+    hop(6)
 
     copies["ru"].wait_recv()
     copies["rd"].wait_recv()
@@ -276,8 +276,9 @@
     edge = dens.at[0:16, 16:24]
     copies["cu"] = push(("cu",), edge, col_in.at[0], {"col": col_of(1)})
     copies["cd"] = push(("cd",), edge, col_in.at[1], {"col": col_of(-1)})
-    ring(7)
-    ring(8)
+    for leaf in (1, -1, 3, -3, 5, -5, 7, -7, 8):
+        for d in order:
+            copies["h", leaf, d].wait_recv()
 
     total = jnp.zeros((256, 128), F32)
     for b in range(NL):

time: 50.6 us -> 48.2 us (0.953)
  the two profiles are of different devices: /device:TPU:32 before, /device:TPU:1 now
where the time goes in v3:
time: 48.2 us; the launch traced here: 48.1 us
  Pallas kernels  45.2 us (94%)
  local copies, waits for them, and re-layouts  2.17 us (5%)
  between operations  0.65 us (1%)
    pallas_call x1, Pallas kernels, on_device(): pl.pallas_call(kernel, out_shape=(jax.ShapeDtypeStruct((256, 128), BF16),...  45.2 us
    unnamed x4, local copies, waits for them, and re-layouts  2.17 us

profile of v3, /device:TPU:1, one launch (start us, length us, event | category | flops | bytes accessed | tf_op | source)
XLA Modules:
  0.0 48.1 jit_solution(7441379519202307884)
XLA Ops:
  0.6 45.2 %shard_map.104 = (bf16[256,128]{1,0:T(8,128)(2,1)}, f32[16,16,128]{2,1,0:T(8,128)}) custom-call(bf16[256,128]{1,0:T(8,128)(2,1)} %bitcast.11, s32[4,8]{1,0:T(4,128)} %bitcast.18, bf16[64,512]{1,0:T(8,128)(2,1)} %bitcast.12, s32[2,16]{1,0:T(2,128)} %bitcast.19, s32[8,128]{1,0:T(8,128)} %bitcast.13, s32[8,128]{1,0:T(8,128)} %bitcast.14, s32[8,128]{1,0:T(8,128)} %bitcast.15, ...), custom_call_target="tpu_custom_call" | custom-call | tf_op jit(solution)/shard_map/pallas_call | solution.py:305
  45.9 0.0 copy-start
  45.9 1.5 %copy.13 = bf16[256,128]{1,0:T(8,128)(2,1)} copy(bf16[256,128]{1,0:T(8,128)(2,1)} %get-tuple-element.4) | data formatting | bytes 131072
  47.4 0.0 copy-done
  47.4 0.7 %copy.14 = f32[16,16,128]{2,1,0:T(8,128)} copy(f32[16,16,128]{2,1,0:T(8,128)S(1)} %copy-done) | data formatting | bytes 262144
Async XLA Ops:
  45.9 1.5 %copy-start = (f32[16,16,128]{2,1,0:T(8,128)S(1)}, f32[16,16,128]{2,1,0:T(8,128)}, u32[]{:S(2)}) copy-start(f32[16,16,128]{2,1,0:T(8,128)} %get-tuple-element.5) | copy-start | bytes 393220

commit v4 on v3

--- a/solution.py
+++ b/solution.py
@@ -22,7 +22,7 @@
 
 def kernel(
     p_hbm, pm_hbm, h_hbm, hm_hbm, row_hbm, gcol_hbm, cell_hbm, expo_hbm, pref_hbm, prod_ref, dens_ref,
-    p_in, pm_in, h_in, hm_in, g_int, g_float, h_ref, turn, pall, hall, gpad, gcols, onehot, colb, acc, ez, plane_hi, plane_lo, dens, rim, rim_in, row_in, col_in,
+    p_in, pm_in, h_in, hm_in, g_int, g_float, h_ref, turn, pall, hall, gpad, gcols, onehot, colb, acc, ez, plane_hi, plane_lo, dens, rim, rim_in, row_in, col_in, side_in,
     send, recv, local,
 ):
     r = lax.axis_index("row")
@@ -51,6 +51,7 @@
         + [{"col": col_of(2 * d)} for d in (1, 2, 3)]
         + [{"col": sib}, {"col": other}]
         + [{"row": row_of(d)} for d in (1, -1, 2, -2)]
+        + [{"row": row_of(a), "layer": lay_of(b)} for a in (1, -1) for b in (1, -1)]
     )
     for peer in peers:
         pl.semaphore_signal(barrier, inc=1, device_id=peer, device_id_type=pl.DeviceIdType.MESH)
@@ -253,24 +254,35 @@
     for k in range(5):
         turned = jnp.transpose(gpad[k * 128 : (k + 1) * 128, :])
         rim[:, k * 128 : (k + 1) * 128] = turned[0:16, :]
-    rim_in[8:120, :] = jnp.zeros((112, 640), F32)
+    for n in range(2):
+        side_in[n, 8:120, :] = jnp.zeros((112, 256), F32)
+    rim_in[8:120, :] = jnp.zeros((112, 384), F32)
     up = {"layer": lay_of(1)}
     down = {"layer": lay_of(-1)}
-    copies["lu"] = push(("lu",), rim.at[0:8], rim_in.at[0:8], up)
-    copies["ld"] = push(("ld",), rim.at[8:16], rim_in.at[120:128], down)
-
-    copies["lu"].wait_recv()
-    copies["ld"].wait_recv()
-    for k in range(5):
-        gpad[k * 128 : (k + 1) * 128, :] = jnp.transpose(rim_in[:, k * 128 : (k + 1) * 128])
-    for k in range(EX):
-        dens[k] = dens[k] + gpad[k * EY : (k + 1) * EY, :]
     copies["ru"] = push(("ru",), dens.at[16:20], row_in.at[0], right)
     copies["rd"] = push(("rd",), dens.at[20:24], row_in.at[1], left)
+    copies["lu"] = push(("lu",), rim.at[0:8, 0:384], rim_in.at[0:8], up)
+    copies["ld"] = push(("ld",), rim.at[8:16, 0:384], rim_in.at[120:128], down)
+    for n, step in enumerate((1, -1)):
+        for name, dz, rows, into in (("u", 1, slice(0, 8), slice(0, 8)), ("d", -1, slice(8, 16), slice(120, 128))):
+            peer = {"row": row_of(step), "layer": lay_of(dz)}
+            copies["s", n, name] = push(("s", n, name), rim.at[rows, 384:640], side_in.at[n, into], peer)
     hop(6)
 
-    copies["ru"].wait_recv()
-    copies["rd"].wait_recv()
+    for k in ("ru", "rd", "lu", "ld"):
+        copies[k].wait_recv()
+    for k in range(3):
+        gpad[k * 128 : (k + 1) * 128, :] = jnp.transpose(rim_in[:, k * 128 : (k + 1) * 128])
+    for k in range(GX):
+        dens[k] = dens[k] + gpad[k * EY : (k + 1) * EY, :]
+    for n, at in ((0, 0), (1, 12)):
+        copies["s", n, "u"].wait_recv()
+        copies["s", n, "d"].wait_recv()
+        for k in range(2):
+            gpad[384 + k * 128 : 512 + k * 128, :] = jnp.transpose(side_in[n, :, k * 128 : (k + 1) * 128])
+        for k in range(4):
+            here = 384 + (n * 4 + k) * EY
+            dens[at + k] = dens[at + k] + gpad[here : here + EY, :]
     dens[0:4] = dens[0:4] + row_in[0]
     dens[12:16] = dens[12:16] + row_in[1]
     edge = dens.at[0:16, 16:24]
@@ -331,9 +343,10 @@
             pltpu.VMEM((EX * EY, NG), BF16),
             pltpu.VMEM((EX, EY, 128), F32),
             pltpu.VMEM((16, 640), F32),
-            pltpu.VMEM((128, 640), F32),
+            pltpu.VMEM((128, 384), F32),
             pltpu.VMEM((2, 4, EY, 128), F32),
             pltpu.VMEM((2, 16, 8, 128), F32),
+            pltpu.VMEM((2, 128, 256), F32),
             pltpu.SemaphoreType.DMA((n_sem,)),
             pltpu.SemaphoreType.DMA((n_sem,)),
             pltpu.SemaphoreType.DMA((11,)),

time: 48.2 us -> 46.3 us (0.961)
  Pallas kernels: 45.2 us -> 43.3 us
    pallas_call x1, Pallas kernels: 45.2 us -> 43.3 us  [on_device(): pl.pallas_call(kernel, out_shape=(jax.ShapeDtypeStruct((256, 128), BF16),...]
where the time goes in v4:
time: 46.3 us; the launch traced here: 46.1 us
  Pallas kernels  43.3 us (94%)
  local copies, waits for them, and re-layouts  2.17 us (5%)
  between operations  0.65 us (1%)
    pallas_call x1, Pallas kernels, on_device(): pl.pallas_call(kernel, out_shape=(jax.ShapeDtypeStruct((256, 128), BF16),...  43.3 us
    unnamed x4, local copies, waits for them, and re-layouts  2.17 us

profile of v4, /device:TPU:1, one launch (start us, length us, event | category | flops | bytes accessed | tf_op | source)
XLA Modules:
  0.0 46.1 jit_solution(18041733452344531314)
XLA Ops:
  0.6 43.3 %shard_map.104 = (bf16[256,128]{1,0:T(8,128)(2,1)}, f32[16,16,128]{2,1,0:T(8,128)}) custom-call(bf16[256,128]{1,0:T(8,128)(2,1)} %bitcast.11, s32[4,8]{1,0:T(4,128)} %bitcast.18, bf16[64,512]{1,0:T(8,128)(2,1)} %bitcast.12, s32[2,16]{1,0:T(2,128)} %bitcast.19, s32[8,128]{1,0:T(8,128)} %bitcast.13, s32[8,128]{1,0:T(8,128)} %bitcast.14, s32[8,128]{1,0:T(8,128)} %bitcast.15, ...), custom_call_target="tpu_custom_call" | custom-call | tf_op jit(solution)/shard_map/pallas_call | solution.py:317
  44.0 0.0 copy-start
  44.0 1.5 %copy.13 = bf16[256,128]{1,0:T(8,128)(2,1)} copy(bf16[256,128]{1,0:T(8,128)(2,1)} %get-tuple-element.4) | data formatting | bytes 131072
  45.5 0.0 copy-done
  45.5 0.7 %copy.14 = f32[16,16,128]{2,1,0:T(8,128)} copy(f32[16,16,128]{2,1,0:T(8,128)S(1)} %copy-done) | data formatting | bytes 262144
Async XLA Ops:
  44.0 1.5 %copy-start = (f32[16,16,128]{2,1,0:T(8,128)S(1)}, f32[16,16,128]{2,1,0:T(8,128)}, u32[]{:S(2)}) copy-start(f32[16,16,128]{2,1,0:T(8,128)} %get-tuple-element.5) | copy-start | bytes 393220

commit v5 on v4

--- a/solution.py
+++ b/solution.py
@@ -230,9 +230,10 @@
     lookup([(col_of(-2 * d), lay_of(-e)) for d, e in corners])
     hop(4)
     for d, e in corners:
-        copies["sa", d, e].wait_recv()
+        copies["sa", e, d].wait_recv()
         copies["sb", d, e].wait_recv()
-    lookup([(sib_of(-2 * d), lay_of(-e)) for d, e in corners])
+        if e == 2:
+            lookup([(sib_of(-2 * d), lay_of(-f)) for f in (1, 3, 2)])
 
     for k in range(NG // 128):
         rows = slice(k * 128, (k + 1) * 128)

time: 46.3 us -> 47.7 us (1.030)
  Pallas kernels: 43.3 us -> 44.7 us
    pallas_call x1, Pallas kernels: 43.3 us -> 44.7 us  [on_device(): pl.pallas_call(kernel, out_shape=(jax.ShapeDtypeStruct((256, 128), BF16),...]
where the time goes in v5:
time: 47.7 us; the launch traced here: 47.5 us
  Pallas kernels  44.7 us (94%)
  local copies, waits for them, and re-layouts  2.17 us (5%)
  between operations  0.65 us (1%)
    pallas_call x1, Pallas kernels, on_device(): pl.pallas_call(kernel, out_shape=(jax.ShapeDtypeStruct((256, 128), BF16),...  44.7 us
    unnamed x4, local copies, waits for them, and re-layouts  2.17 us

profile of v5, /device:TPU:1, one launch (start us, length us, event | category | flops | bytes accessed | tf_op | source)
XLA Modules:
  0.0 47.5 jit_solution(13935047288846783923)
XLA Ops:
  0.6 44.7 %shard_map.104 = (bf16[256,128]{1,0:T(8,128)(2,1)}, f32[16,16,128]{2,1,0:T(8,128)}) custom-call(bf16[256,128]{1,0:T(8,128)(2,1)} %bitcast.11, s32[4,8]{1,0:T(4,128)} %bitcast.18, bf16[64,512]{1,0:T(8,128)(2,1)} %bitcast.12, s32[2,16]{1,0:T(2,128)} %bitcast.19, s32[8,128]{1,0:T(8,128)} %bitcast.13, s32[8,128]{1,0:T(8,128)} %bitcast.14, s32[8,128]{1,0:T(8,128)} %bitcast.15, ...), custom_call_target="tpu_custom_call" | custom-call | tf_op jit(solution)/shard_map/pallas_call | solution.py:318
  45.3 0.0 copy-start
  45.3 1.5 %copy.13 = bf16[256,128]{1,0:T(8,128)(2,1)} copy(bf16[256,128]{1,0:T(8,128)(2,1)} %get-tuple-element.4) | data formatting | bytes 131072
  46.8 0.0 copy-done
  46.9 0.7 %copy.14 = f32[16,16,128]{2,1,0:T(8,128)} copy(f32[16,16,128]{2,1,0:T(8,128)S(1)} %copy-done) | data formatting | bytes 262144
Async XLA Ops:
  45.3 1.5 %copy-start = (f32[16,16,128]{2,1,0:T(8,128)S(1)}, f32[16,16,128]{2,1,0:T(8,128)}, u32[]{:S(2)}) copy-start(f32[16,16,128]{2,1,0:T(8,128)} %get-tuple-element.5) | copy-start | bytes 393220
